TPU v7x, 256 devices: a whole 4x4x8 slice. The times are simulated.
256 devices in a mesh: seq: 64 (over z, y, core), ch: 4 (over x).
Axes of the slice: x: 4, y: 4, z: 8, core: 2. Of those that a mesh axis runs over, the one named last changes fastest.
Arguments:
- query_proj: bfloat16 [8192, 2048], P('seq', 'ch'), may hold values from -6 to 6
- key_proj: bfloat16 [8192, 2048], P('seq', 'ch'), may hold values from -6 to 6
- value_proj: bfloat16 [8192, 2048], P('seq', 'ch'), may hold values from -6 to 6
- short_filter: float32 [3, 3, 2048], P(None, None, 'ch'), may hold values from -3.5 to 3.5
- long_filter: float32 [8192, 2048], P('seq', 'ch'), may hold values from -0.0625 to 0.0625
- skip_gain: float32 [2048], P('ch'), may hold values from 0.5 to 1.5
- out_weight: bfloat16 [2048, 4096], P('ch'), may hold values from -0.125 to 0.125
- cotangent: bfloat16 [8192, 4096], P('seq', 'ch'), may hold values from -16 to 16
Outputs:
- layer_out: bfloat16 [8192, 4096], P('seq', 'ch')
- grad_query: float32 [8192, 2048], P('seq', 'ch')
- grad_key: float32 [8192, 2048], P('seq', 'ch')
- grad_value: float32 [8192, 2048], P('seq', 'ch')
- grad_short: float32 [3, 3, 2048], P(None, None, 'ch')
- grad_filter: float32 [8192, 2048], P('seq', 'ch')
- grad_skip: float32 [2048], P('ch')
- grad_w_out_t: float32 [4096, 2048], P('seq', 'ch')
All inputs are finite; a program needn't handle non-finite values.
Results may differ from a plain program's by a relative error of at most 0.011.
Values may be sent and summed in bfloat16 or wider, within the bound.
A program may use at most 128 MiB of HBM per device.

v0:
```python
import math
import jax
import jax.numpy as jnp
from jax import lax
from jax.sharding import PartitionSpec as P

exact_mode = lax.Precision.HIGHEST


def from_behind(shard, axis, by):
    size = lax.axis_size(axis)
    pairs = [(i, i + by) for i in range(size) if 0 <= i + by < size]
    return lax.ppermute(shard, axis, pairs)


def as_sent(shard):

    def short(part):
        return part.astype(jnp.bfloat16) if part.dtype == jnp.float32 else part

    return jax.tree.map(short, shard)


def tables(rows_out, cols_in, period):
    row_index = lax.broadcasted_iota(jnp.int32, (rows_out, cols_in), 0)
    col_index = lax.broadcasted_iota(jnp.int32, (rows_out, cols_in), 1)
    phase_angle = (row_index * col_index % period).astype(jnp.float32) * (2.0 * math.pi / period)
    return (jnp.cos(phase_angle), jnp.sin(phase_angle))


def along_rows(factor, values):
    return jnp.tensordot(factor, values, axes=1, precision=exact_mode)


def rows_spectrum(signal, basis_pair):
    return (along_rows(basis_pair[0], signal), -along_rows(basis_pair[1], signal))


def rows_inverse(complex_pair, basis_pair):
    total = along_rows(basis_pair[0], complex_pair[0]) - along_rows(basis_pair[1], complex_pair[1])
    return total / basis_pair[0].shape[1]


def block_forward(complex_pair, basis_pair):
    cosine_part, sine_part = basis_pair
    real_part = along_rows(cosine_part, complex_pair[0]) + along_rows(sine_part, complex_pair[1])
    imag_part = along_rows(cosine_part, complex_pair[1]) - along_rows(sine_part, complex_pair[0])
    return (real_part, imag_part)


def block_inverse(complex_pair, basis_pair):
    cosine_part, sine_part = basis_pair
    norming = 1.0 / cosine_part.shape[1]
    real_part = along_rows(cosine_part, complex_pair[0]) - along_rows(sine_part, complex_pair[1])
    imag_part = along_rows(cosine_part, complex_pair[1]) + along_rows(sine_part, complex_pair[0])
    return (real_part * norming, imag_part * norming)


def complex_product(first_pair, second_pair):
    return (
        first_pair[0] * second_pair[0] - first_pair[1] * second_pair[1],
        first_pair[0] * second_pair[1] + first_pair[1] * second_pair[0],
    )


def conj_product(first_pair, second_pair):
    return (
        first_pair[0] * second_pair[0] + first_pair[1] * second_pair[1],
        first_pair[0] * second_pair[1] - first_pair[1] * second_pair[0],
    )


def on_device(
    query_proj, key_proj, value_proj, short_filter, long_filter, skip_gain, out_weight, cotangent
):
    block_rows = query_proj.shape[0]
    tap_count = short_filter.shape[1]
    block_count = lax.axis_size("seq")
    streams = jnp.stack([query_proj, key_proj, value_proj])
    earlier = from_behind(streams[:, block_rows - (tap_count - 1) :], "seq", 1)
    extended = jnp.concatenate([earlier, streams], axis=1).astype(jnp.float32)
    shifted = [
        extended[:, tap_count - 1 - offset : tap_count - 1 - offset + block_rows]
        for offset in range(tap_count)
    ]
    filtered = sum(
        (short_filter[:, offset][:, None, :] * shifted[offset] for offset in range(tap_count))
    )
    query_short, key_short, value_short = (filtered[0], filtered[1], filtered[2])
    product = key_short * value_short
    forward_basis = tables(2 * block_rows, block_rows, 2 * block_rows)
    full_basis = tables(2 * block_rows, 2 * block_rows, 2 * block_rows)
    half_basis = tables(block_rows, 2 * block_rows, 2 * block_rows)
    block_basis = tables(2 * block_count, block_count, 2 * block_count)
    return_basis = tables(block_count, 2 * block_count, 2 * block_count)
    input_pair = rows_spectrum(product, forward_basis)
    filter_pair = rows_spectrum(long_filter, forward_basis)
    moved_data = (
        lax.all_to_all(input_pair[0][None], "seq", split_axis=1, concat_axis=0, tiled=True),
        lax.all_to_all(input_pair[1][None], "seq", split_axis=1, concat_axis=0, tiled=True),
        lax.all_to_all(filter_pair[0][None], "seq", split_axis=1, concat_axis=0, tiled=True),
        lax.all_to_all(filter_pair[1][None], "seq", split_axis=1, concat_axis=0, tiled=True),
    )
    input_spectrum = block_forward((moved_data[0], moved_data[1]), block_basis)
    filter_spectrum = block_forward((moved_data[2], moved_data[3]), block_basis)
    inverse_pair = block_inverse(complex_product(filter_spectrum, input_spectrum), return_basis)
    returned = (
        lax.all_to_all(inverse_pair[0], "seq", split_axis=0, concat_axis=1, tiled=True),
        lax.all_to_all(inverse_pair[1], "seq", split_axis=0, concat_axis=1, tiled=True),
    )
    folded = rows_inverse((returned[0][0], returned[1][0]), full_basis)
    carried = from_behind(folded[block_rows:], "seq", 1)
    convolved = folded[:block_rows] + carried
    mixed_seq = convolved + skip_gain * product
    gated_values = (query_short * mixed_seq).astype(jnp.bfloat16)
    partial_value = jnp.dot(gated_values, out_weight, preferred_element_type=jnp.float32)
    layer_out = lax.psum_scatter(partial_value, "ch", scatter_dimension=1, tiled=True).astype(
        jnp.bfloat16
    )
    full_cotangent = lax.all_gather(cotangent, "ch", axis=1, tiled=True)
    grad_gated = lax.dot_general(
        full_cotangent, out_weight, (((1,), (1,)), ((), ())), preferred_element_type=jnp.float32
    )
    grad_w_out_t = lax.psum_scatter(
        lax.dot_general(
            full_cotangent,
            gated_values,
            (((0,), (0,)), ((), ())),
            preferred_element_type=jnp.float32,
        ),
        "seq",
        scatter_dimension=0,
        tiled=True,
    )
    grad_mixed = grad_gated * query_short
    grad_query_short = grad_gated * mixed_seq
    following = from_behind(grad_mixed.astype(jnp.bfloat16), "seq", -1).astype(grad_mixed.dtype)
    spread = jnp.concatenate([grad_mixed, following], axis=0)
    grad_pair = rows_spectrum(spread, full_basis)
    moved_grad = (
        lax.all_to_all(
            grad_pair[0][None].astype(jnp.bfloat16), "seq", split_axis=1, concat_axis=0, tiled=True
        ).astype(jnp.float32),
        lax.all_to_all(
            grad_pair[1][None].astype(jnp.bfloat16), "seq", split_axis=1, concat_axis=0, tiled=True
        ).astype(jnp.float32),
    )
    grad_spectrum = block_forward(moved_grad, block_basis)
    input_back = block_inverse(conj_product(filter_spectrum, grad_spectrum), return_basis)
    filter_back = block_inverse(conj_product(input_spectrum, grad_spectrum), return_basis)
    returned_grad = (
        lax.all_to_all(as_sent(input_back[0]), "seq", split_axis=0, concat_axis=1, tiled=True),
        lax.all_to_all(as_sent(input_back[1]), "seq", split_axis=0, concat_axis=1, tiled=True),
        lax.all_to_all(as_sent(filter_back[0]), "seq", split_axis=0, concat_axis=1, tiled=True),
        lax.all_to_all(as_sent(filter_back[1]), "seq", split_axis=0, concat_axis=1, tiled=True),
    )
    conv_grad = rows_inverse((returned_grad[0][0], returned_grad[1][0]), half_basis)
    grad_filter = rows_inverse((returned_grad[2][0], returned_grad[3][0]), half_basis)
    grad_product = conv_grad + skip_gain * grad_mixed
    grad_streams = jnp.stack(
        [grad_query_short, grad_product * value_short, grad_product * key_short]
    )
    later_rows = from_behind(grad_streams[:, : tap_count - 1], "seq", -1)
    padded_grad = jnp.concatenate([grad_streams, later_rows], axis=1)
    grad_inputs = sum(
        (
            short_filter[:, offset][:, None, :] * padded_grad[:, offset : offset + block_rows]
            for offset in range(tap_count)
        )
    )
    short_terms = jnp.stack(
        [jnp.sum(grad_streams * shifted[offset], axis=1) for offset in range(tap_count)], axis=1
    )
    skip_terms = jnp.sum(grad_mixed * product, axis=0)
    grad_short, grad_skip = lax.psum((short_terms, skip_terms), "seq")
    return (
        layer_out,
        grad_inputs[0],
        grad_inputs[1],
        grad_inputs[2],
        grad_short,
        grad_filter,
        grad_skip,
        grad_w_out_t,
    )


def solution(mesh):
    in_specs = (
        P("seq", "ch"),
        P("seq", "ch"),
        P("seq", "ch"),
        P(None, None, "ch"),
        P("seq", "ch"),
        P("ch"),
        P("ch", None),
        P("seq", "ch"),
    )
    out_specs = (
        P("seq", "ch"),
        P("seq", "ch"),
        P("seq", "ch"),
        P("seq", "ch"),
        P(None, None, "ch"),
        P("seq", "ch"),
        P("ch"),
        P("seq", "ch"),
    )
    return jax.shard_map(
        on_device, mesh=mesh, in_specs=in_specs, out_specs=out_specs, check_vma=False
    )
```

profile of v0, /device:TPU:128, one launch (start us, length us, event | category | flops | bytes accessed | tf_op | source)
XLA Modules:
  0.0 595.5 jit_solution(4163369998278943151)
XLA Ops:
  10.5 10.5 %all-to-all-start.1 = ((f32[1,256,512]{2,0,1:T(1,128)}), f32[1,256,512]{2,0,1:T(1,128)S(1)}, u32[]{:S(2)}, u32[]{:S(2)}) async-start(f32[1,256,512]{2,0,1:T(1,128)} %copy.65), calls=%async_computation.1 | async-start | bytes 1048576 | tf_op jit(solution)/shard_map/all_to_all | solution.py:102
  22.5 2.1 collective-permute-start
  27.0 8.9 %all-to-all-done.1 = f32[1,256,512]{2,0,1:T(1,128)S(1)} async-done(((f32[1,256,512]{2,0,1:T(1,128)}), f32[1,256,512]{2,0,1:T(1,128)S(1)}, u32[]{:S(2)}, u32[]{:S(2)}) %all-to-all-start.1) | async-done | bytes 524320 | tf_op jit(solution)/shard_map/all_to_all | solution.py:102
  35.9 8.6 %all-to-all-start = ((f32[1,256,512]{2,0,1:T(1,128)}), f32[1,256,512]{2,0,1:T(1,128)S(1)}, u32[]{:S(2)}, u32[]{:S(2)}) async-start(f32[1,256,512]{2,0,1:T(1,128)} %copy.63), calls=%async_computation | async-start | bytes 1048576 | tf_op jit(solution)/shard_map/all_to_all | solution.py:101
  44.9 6.6 %all-gather.2.cloned.1.call-done = bf16[128,4096]{1,0:T(8,128)(2,1)} async-done(((bf16[128,1024]{1,0:T(8,128)(2,1)}), bf16[128,4096]{1,0:T(8,128)(2,1)}) %all-gather.2.cloned.1.call-update) | async-done | bytes 1048592 | tf_op jit(solution)/shard_map/all_gather | solution.py:120
  51.5 4.8 multiply_reduce_fusion.3
  56.3 3.1 collective-permute-start.2
  59.4 2.5 collective-permute-done.2
  62.6 1.6 fusion.14
  65.2 2.2 reduce.8
  68.3 12.3 %all-to-all-start.6 = ((bf16[64,2,1024]{2,1,0:T(2,128)(2,1)}), bf16[64,2,1024]{2,1,0:T(2,128)(2,1)}, u32[]{:S(2)}, u32[]{:S(2)}) async-start(bf16[64,2,1024]{2,1,0:T(2,128)(2,1)} %reshape.75), calls=%async_computation.7 | async-start | bytes 524288 | tf_op jit(solution)/shard_map/all_to_all | solution.py:141
  82.0 2.6 fusion.15
  85.0 2.2 reduce.9
  88.1 1.5 all-to-all-done.6
  89.6 9.1 %all-to-all-start.7 = ((bf16[64,2,1024]{2,1,0:T(2,128)(2,1)}), bf16[64,2,1024]{2,1,0:T(2,128)(2,1)}, u32[]{:S(2)}, u32[]{:S(2)}) async-start(bf16[64,2,1024]{2,1,0:T(2,128)(2,1)} %reshape.73), calls=%async_computation.8 | async-start | bytes 524288 | tf_op jit(solution)/shard_map/all_to_all | solution.py:144
  99.9 2.1 reduce.1
  103.3 2.1 convolution_add_fusion.2
  107.9 10.4 %all-to-all-start.3 = ((f32[1,256,512]{2,0,1:T(1,128)}), f32[1,256,512]{2,0,1:T(1,128)S(1)}, u32[]{:S(2)}, u32[]{:S(2)}) async-start(f32[1,256,512]{2,0,1:T(1,128)} %copy.69), calls=%async_computation.3 | async-start | bytes 1048576 | tf_op jit(solution)/shard_map/all_to_all | solution.py:100
  119.5 2.2 convolution_subtract_fusion.2
  124.0 2.1 reshape.76
  126.2 1.5 bitcast_reduce_fusion
  127.7 2.1 reshape.74
  129.9 1.5 bitcast_reduce_fusion.1
  131.5 1.7 all-to-all-done.3
  133.2 8.8 %all-to-all-start.2 = ((f32[1,256,512]{2,0,1:T(1,128)}), f32[1,256,512]{2,0,1:T(1,128)S(1)}, u32[]{:S(2)}, u32[]{:S(2)}) async-start(f32[1,256,512]{2,0,1:T(1,128)} %copy.67), calls=%async_computation.2 | async-start | bytes 1048576 | tf_op jit(solution)/shard_map/all_to_all | solution.py:99
  143.5 1.7 convolution_subtract_fusion
  145.3 1.7 convolution_add_fusion
  148.4 8.3 %all-to-all-done.2 = f32[1,256,512]{2,0,1:T(1,128)S(1)} async-done(((f32[1,256,512]{2,0,1:T(1,128)}), f32[1,256,512]{2,0,1:T(1,128)S(1)}, u32[]{:S(2)}, u32[]{:S(2)}) %all-to-all-start.2) | async-done | bytes 524320 | tf_op jit(solution)/shard_map/all_to_all | solution.py:99
  161.6 5.8 multiply_subtract_fusion
  171.4 8.7 %all-to-all-start.8 = ((bf16[64,4,512]{2,1,0:T(4,128)(2,1)}), bf16[64,4,512]{2,1,0:T(4,128)(2,1)}, u32[]{:S(2)}, u32[]{:S(2)}) async-start(bf16[64,4,512]{2,1,0:T(4,128)(2,1)} %copy.83), calls=%async_computation.9 | async-start | bytes 524288 | tf_op jit(solution)/shard_map/all_to_all | solution.py:152
  180.1 2.0 fusion.115
  182.1 2.0 fusion.5
  185.3 4.0 all-to-all-done.8
  189.3 9.1 %all-to-all-start.4 = ((f32[64,4,512]{2,1,0:T(4,128)}), f32[64,4,512]{2,1,0:T(4,128)}, u32[]{:S(2)}, u32[]{:S(2)}) async-start(f32[64,4,512]{2,1,0:T(4,128)} %copy.75), calls=%async_computation.4 | async-start | bytes 1048576 | tf_op jit(solution)/shard_map/all_to_all | solution.py:108
  198.4 2.0 fusion.113
  200.4 2.0 fusion.4
  203.6 9.7 %all-to-all-done.4 = f32[64,4,512]{2,1,0:T(4,128)} async-done(((f32[64,4,512]{2,1,0:T(4,128)}), f32[64,4,512]{2,1,0:T(4,128)}, u32[]{:S(2)}, u32[]{:S(2)}) %all-to-all-start.4) | async-done | bytes 524320 | tf_op jit(solution)/shard_map/all_to_all | solution.py:108
  213.3 8.7 %all-to-all-start.5 = ((f32[64,4,512]{2,1,0:T(4,128)}), f32[64,4,512]{2,1,0:T(4,128)}, u32[]{:S(2)}, u32[]{:S(2)}) async-start(f32[64,4,512]{2,1,0:T(4,128)} %copy.76), calls=%async_computation.5 | async-start | bytes 1048576 | tf_op jit(solution)/shard_map/all_to_all | solution.py:109
  222.8 2.0 fusion.11
  225.7 1.7 squeeze.41
  227.4 2.1 squeeze.39
  229.5 7.3 %all-to-all-done.5 = f32[64,4,512]{2,1,0:T(4,128)} async-done(((f32[64,4,512]{2,1,0:T(4,128)}), f32[64,4,512]{2,1,0:T(4,128)}, u32[]{:S(2)}, u32[]{:S(2)}) %all-to-all-start.5) | async-done | bytes 524320 | tf_op jit(solution)/shard_map/all_to_all | solution.py:109
  236.8 8.7 %all-to-all-start.9 = ((bf16[64,4,512]{2,1,0:T(4,128)(2,1)}), bf16[64,4,512]{2,1,0:T(4,128)(2,1)}, u32[]{:S(2)}, u32[]{:S(2)}) async-start(bf16[64,4,512]{2,1,0:T(4,128)(2,1)} %copy.84), calls=%async_computation.10 | async-start | bytes 524288 | tf_op jit(solution)/shard_map/all_to_all | solution.py:153
  245.7 3.5 fusion.61
  249.3 2.0 squeeze.40
  251.3 2.8 fusion.8
  255.6 2.0 collective-permute-start.1
  257.7 2.4 fusion.71
  260.1 1.7 squeeze.42
  261.8 1.9 fusion.18
  263.8 3.2 collective-permute-done.1
  267.0 1.8 multiply_bitcast_fusion.2
  269.6 2.0 fusion.301
  271.7 5.4 convolution_bitcast_fusion
  277.1 9.1 %copy.89 = f32[4096,512]{1,0:T(8,128)} copy(f32[4096,512]{0,1:T(8,128)} %convolution_bitcast_fusion) | data formatting | bytes 16777216
  289.1 8.5 %all-to-all-start.11 = ((bf16[64,4,512]{2,1,0:T(4,128)(2,1)}), bf16[64,4,512]{2,1,0:T(4,128)(2,1)}, u32[]{:S(2)}, u32[]{:S(2)}) async-start(bf16[64,4,512]{2,1,0:T(4,128)(2,1)} %copy.86), calls=%async_computation.12 | async-start | bytes 524288 | tf_op jit(solution)/shard_map/all_to_all | solution.py:155
  300.2 6.4 %all-to-all-done.11 = bf16[64,4,512]{2,1,0:T(4,128)(2,1)} async-done(((bf16[64,4,512]{2,1,0:T(4,128)(2,1)}), bf16[64,4,512]{2,1,0:T(4,128)(2,1)}, u32[]{:S(2)}, u32[]{:S(2)}) %all-to-all-start.11) | async-done | bytes 262176 | tf_op jit(solution)/shard_map/all_to_all | solution.py:155
  306.6 8.6 %all-to-all-start.10 = ((bf16[64,4,512]{2,1,0:T(4,128)(2,1)}), bf16[64,4,512]{2,1,0:T(4,128)(2,1)S(1)}, u32[]{:S(2)}, u32[]{:S(2)}) async-start(bf16[64,4,512]{2,1,0:T(4,128)(2,1)} %copy.85), calls=%async_computation.11 | async-start | bytes 524288 | tf_op jit(solution)/shard_map/all_to_all | solution.py:154
  316.3 8.2 %all-to-all-done.10 = bf16[64,4,512]{2,1,0:T(4,128)(2,1)S(1)} async-done(((bf16[64,4,512]{2,1,0:T(4,128)(2,1)}), bf16[64,4,512]{2,1,0:T(4,128)(2,1)S(1)}, u32[]{:S(2)}, u32[]{:S(2)}) %all-to-all-start.10) | async-done | bytes 262176 | tf_op jit(solution)/shard_map/all_to_all | solution.py:154
  325.4 4.2 collective-permute-start.3
  329.7 1.5 fusion.16
  332.2 1.5 multiply_reduce_fusion.2
  333.7 251.7 %all-reduce = (f32[3,3,512]{2,0,1:T(4,128)S(1)}, f32[512]{0:T(512)}) all-reduce(f32[3,3,512]{2,0,1:T(4,128)S(1)} %pad_maximum_fusion.5, f32[512]{0:T(512)S(1)} %get-tuple-element.45), channel_id=1, replica_groups=mesh['seq'=64,'ch'=4] {'seq'}, use_global_device_ids=true, to_apply=%region_4.5 | all-reduce | flops 5120 | bytes 40960 | tf_op jit(solution)/shard_map/psum | solution.py:175
  586.9 1.8 convert_element_type.124
  (118 shorter events, 49.4 us)
Async XLA Ops:
  7.2 1.0 copy-start
  7.2 37.3 %copy-start.16 = (bf16[128,512]{1,0:T(8,128)(2,1)S(1)}, bf16[128,512]{1,0:T(8,128)(2,1)}, u32[]{:S(2)}) copy-start(bf16[128,512]{1,0:T(8,128)(2,1)} %param.10) | copy-start | bytes 393220
  7.2 37.3 %copy-start.17 = (bf16[128,512]{1,0:T(8,128)(2,1)S(1)}, bf16[128,512]{1,0:T(8,128)(2,1)}, u32[]{:S(2)}) copy-start(bf16[128,512]{1,0:T(8,128)(2,1)} %param.9) | copy-start | bytes 393220
  7.2 37.3 %copy-start.18 = (bf16[128,512]{1,0:T(8,128)(2,1)S(1)}, bf16[128,512]{1,0:T(8,128)(2,1)}, u32[]{:S(2)}) copy-start(bf16[128,512]{1,0:T(8,128)(2,1)} %param.8) | copy-start | bytes 393220
  7.2 19.8 %copy-start.20 = (f32[3,3,512]{2,1,0:T(4,128)S(1)}, f32[3,3,512]{2,1,0:T(4,128)}, u32[]{:S(2)}) copy-start(f32[3,3,512]{2,1,0:T(4,128)} %param.11) | copy-start | bytes 55300
  10.5 25.4 %all-to-all-start.1 = ((f32[1,256,512]{2,0,1:T(1,128)}), f32[1,256,512]{2,0,1:T(1,128)S(1)}, u32[]{:S(2)}, u32[]{:S(2)}) async-start(f32[1,256,512]{2,0,1:T(1,128)} %copy.65), calls=%async_computation.1 | async-start | bytes 1048576 | tf_op jit(solution)/shard_map/all_to_all | solution.py:102
  21.0 30.5 %all-gather.2.cloned.1.call-start = ((), (), s32[]{:S(2)}) async-start(), calls=%async_computation.15 | async-start | bytes 1310720 | tf_op jit(solution)/shard_map/all_gather | solution.py:120
  22.5 22.0 %collective-permute-start = (bf16[3,2,512]{2,1,0:T(2,128)(2,1)S(1)}, bf16[3,2,512]{2,1,0:T(2,128)(2,1)S(1)}, u32[]{:S(2)}, u32[]{:S(2)}) collective-permute-start(bf16[3,2,512]{2,1,0:T(2,128)(2,1)S(1)} %pad_maximum_fusion.6), channel_id=1, source_target_pairs={{0,4},{4,8},{8,12},{12,16},{16,20},{20,24},{24,28},{28,32},{32,36}... | collective-permute-start | bytes 18440 | tf_op jit(solution)/shard_map/ppermute | solution.py:13
  35.9 8.6 %copy-start.12 = (f32[1,256,512]{2,0,1:T(1,128)}, f32[1,256,512]{2,0,1:T(1,128)S(1)}, u32[]{:S(2)}) copy-start(f32[1,256,512]{2,0,1:T(1,128)S(1)} %all-to-all-done.1) | copy-start | bytes 1572868
  35.9 32.4 %all-to-all-start = ((f32[1,256,512]{2,0,1:T(1,128)}), f32[1,256,512]{2,0,1:T(1,128)S(1)}, u32[]{:S(2)}, u32[]{:S(2)}) async-start(f32[1,256,512]{2,0,1:T(1,128)} %copy.63), calls=%async_computation | async-start | bytes 1048576 | tf_op jit(solution)/shard_map/all_to_all | solution.py:101
  44.9 19.3 %copy-start.6 = (f32[3,128,512]{2,1,0:T(8,128)}, f32[3,128,512]{2,1,0:T(8,128)S(1)}, u32[]{:S(2)}) copy-start(f32[3,128,512]{2,1,0:T(8,128)S(1)} %multiply_add_fusion.3) | copy-start | bytes 2359300
  56.3 5.6 collective-permute-start.2
  61.9 0.7 copy-start.19
  68.3 31.6 %copy-start.13 = (f32[1,256,512]{2,0,1:T(1,128)S(1)}, f32[1,256,512]{2,0,1:T(1,128)}, u32[]{:S(2)}) copy-start(f32[1,256,512]{2,0,1:T(1,128)} %copy-done.12) | copy-start | bytes 1572868
  68.3 21.3 %all-to-all-start.6 = ((bf16[64,2,1024]{2,1,0:T(2,128)(2,1)}), bf16[64,2,1024]{2,1,0:T(2,128)(2,1)}, u32[]{:S(2)}, u32[]{:S(2)}) async-start(bf16[64,2,1024]{2,1,0:T(2,128)(2,1)} %reshape.75), calls=%async_computation.7 | async-start | bytes 524288 | tf_op jit(solution)/shard_map/all_to_all | solution.py:141
  89.6 18.3 %all-to-all-start.7 = ((bf16[64,2,1024]{2,1,0:T(2,128)(2,1)}), bf16[64,2,1024]{2,1,0:T(2,128)(2,1)}, u32[]{:S(2)}, u32[]{:S(2)}) async-start(bf16[64,2,1024]{2,1,0:T(2,128)(2,1)} %reshape.73), calls=%async_computation.8 | async-start | bytes 524288 | tf_op jit(solution)/shard_map/all_to_all | solution.py:144
  107.9 25.3 %all-to-all-start.3 = ((f32[1,256,512]{2,0,1:T(1,128)}), f32[1,256,512]{2,0,1:T(1,128)S(1)}, u32[]{:S(2)}, u32[]{:S(2)}) async-start(f32[1,256,512]{2,0,1:T(1,128)} %copy.69), calls=%async_computation.3 | async-start | bytes 1048576 | tf_op jit(solution)/shard_map/all_to_all | solution.py:100
  133.2 23.5 %all-to-all-start.2 = ((f32[1,256,512]{2,0,1:T(1,128)}), f32[1,256,512]{2,0,1:T(1,128)S(1)}, u32[]{:S(2)}, u32[]{:S(2)}) async-start(f32[1,256,512]{2,0,1:T(1,128)} %copy.67), calls=%async_computation.2 | async-start | bytes 1048576 | tf_op jit(solution)/shard_map/all_to_all | solution.py:99
  158.1 2.4 copy-start.5
  167.4 1.0 copy-start.4
  171.4 17.9 %all-to-all-start.8 = ((bf16[64,4,512]{2,1,0:T(4,128)(2,1)}), bf16[64,4,512]{2,1,0:T(4,128)(2,1)}, u32[]{:S(2)}, u32[]{:S(2)}) async-start(bf16[64,4,512]{2,1,0:T(4,128)(2,1)} %copy.83), calls=%async_computation.9 | async-start | bytes 524288 | tf_op jit(solution)/shard_map/all_to_all | solution.py:152
  189.3 24.0 %all-to-all-start.4 = ((f32[64,4,512]{2,1,0:T(4,128)}), f32[64,4,512]{2,1,0:T(4,128)}, u32[]{:S(2)}, u32[]{:S(2)}) async-start(f32[64,4,512]{2,1,0:T(4,128)} %copy.75), calls=%async_computation.4 | async-start | bytes 1048576 | tf_op jit(solution)/shard_map/all_to_all | solution.py:108
  213.3 23.5 %all-to-all-start.5 = ((f32[64,4,512]{2,1,0:T(4,128)}), f32[64,4,512]{2,1,0:T(4,128)}, u32[]{:S(2)}, u32[]{:S(2)}) async-start(f32[64,4,512]{2,1,0:T(4,128)} %copy.76), calls=%async_computation.5 | async-start | bytes 1048576 | tf_op jit(solution)/shard_map/all_to_all | solution.py:109
  224.8 37.0 %copy-start.21 = (f32[512]{0:T(512)S(1)}, f32[512]{0:T(512)}, u32[]{:S(2)}) copy-start(f32[512]{0:T(512)} %param.13) | copy-start | bytes 6148
  227.4 39.5 %copy-start.15 = (f32[128,512]{1,0:T(8,128)S(1)}, f32[128,512]{1,0:T(8,128)}, u32[]{:S(2)}) copy-start(f32[128,512]{1,0:T(8,128)} %get-tuple-element.70) | copy-start | bytes 786436
  236.8 23.3 %all-to-all-start.9 = ((bf16[64,4,512]{2,1,0:T(4,128)(2,1)}), bf16[64,4,512]{2,1,0:T(4,128)(2,1)}, u32[]{:S(2)}, u32[]{:S(2)}) async-start(bf16[64,4,512]{2,1,0:T(4,128)(2,1)} %copy.84), calls=%async_computation.10 | async-start | bytes 524288 | tf_op jit(solution)/shard_map/all_to_all | solution.py:153
  245.5 23.3 %copy-start.7 = (f32[3,128,512]{2,1,0:T(8,128)S(1)}, f32[3,128,512]{2,1,0:T(8,128)}, u32[]{:S(2)}) copy-start(f32[3,128,512]{2,1,0:T(8,128)} %copy-done.6) | copy-start | bytes 2359300
  245.5 341.4 %reduce-scatter.5.cloned.1.call-start = ((), (), s32[]{:S(2)}) async-start(), calls=%async_computation.14 | async-start | bytes 2621440 | tf_op jit(solution)/shard_map/reduce_scatter | solution.py:117
  254.1 0.8 copy-start.11
  255.6 11.3 %collective-permute-start.1 = (f32[128,512]{1,0:T(8,128)}, f32[128,512]{1,0:T(8,128)}, u32[]{:S(2)}, u32[]{:S(2)}) collective-permute-start(f32[128,512]{1,0:T(8,128)} %slice.82), channel_id=1, source_target_pairs={{0,4},{4,8},{8,12},{12,16},{16,20},{20,24},{24,28},{28,32},{32,36}... | collective-permute-start | bytes 786440 | tf_op jit(solution)/shard_map/ppermute | solution.py:13
  261.8 7.7 %copy-start.2 = (bf16[512,4096]{1,0:T(8,128)(2,1)S(1)}, bf16[512,4096]{1,0:T(8,128)(2,1)}, u32[]{:S(2)}) copy-start(bf16[512,4096]{1,0:T(8,128)(2,1)} %param.14) | copy-start | bytes 12582916
  268.9 0.7 copy-start.14
  268.9 56.4 %copy-start.9 = (f32[1,128,512]{2,1,0:T(8,128)}, f32[1,128,512]{2,1,0:T(8,128)S(1)}, u32[]{:S(2)}) copy-start(f32[1,128,512]{2,1,0:T(8,128)S(1)} %get-tuple-element.61) | copy-start | bytes 786436
  269.6 2.1 copy-start.8
  271.6 317.0 %reduce-scatter.7.cloned.1.call-start = ((), (), s32[]{:S(2)}) async-start(), calls=%async_computation.16 | async-start | bytes 8519680
  286.2 1.2 copy-start.3
  289.1 17.5 %all-to-all-start.11 = ((bf16[64,4,512]{2,1,0:T(4,128)(2,1)}), bf16[64,4,512]{2,1,0:T(4,128)(2,1)}, u32[]{:S(2)}, u32[]{:S(2)}) async-start(bf16[64,4,512]{2,1,0:T(4,128)(2,1)} %copy.86), calls=%async_computation.12 | async-start | bytes 524288 | tf_op jit(solution)/shard_map/all_to_all | solution.py:155
  298.5 26.9 %copy-start.10 = (f32[1,128,512]{2,1,0:T(8,128)S(1)}, f32[1,128,512]{2,1,0:T(8,128)}, u32[]{:S(2)}) copy-start(f32[1,128,512]{2,1,0:T(8,128)} %get-tuple-element.48) | copy-start | bytes 786436
  306.6 17.9 %all-to-all-start.10 = ((bf16[64,4,512]{2,1,0:T(4,128)(2,1)}), bf16[64,4,512]{2,1,0:T(4,128)(2,1)S(1)}, u32[]{:S(2)}, u32[]{:S(2)}) async-start(bf16[64,4,512]{2,1,0:T(4,128)(2,1)} %copy.85), calls=%async_computation.11 | async-start | bytes 524288 | tf_op jit(solution)/shard_map/all_to_all | solution.py:154
  325.4 5.7 collective-permute-start.3
  331.1 257.6 %copy-start.1 = (f32[128,512]{1,0:T(8,128)S(1)}, f32[128,512]{1,0:T(8,128)}, u32[]{:S(2)}) copy-start(f32[128,512]{1,0:T(8,128)} %param.12) | copy-start | bytes 786436
Sparse Core Ops, SparseCore 0:
  23.7 27.7 all-gather.1
  271.8 30.2 reduce-scatter.4
  307.4 149.4 reduce-scatter.6
where the time goes:
time: 606 us; the launch traced here: 595 us
  blocking collectives  252 us (42%)
  starting transfers between devices  124 us (20%)
  matrix products  70.6 us (12%)
  waiting for transfers between devices  69 us (11%)
  local copies, waits for them, and re-layouts  47.8 us (8%)
  other arithmetic  17.7 us (3%)
  between operations  14.7 us (2%)
    psum x1, blocking collectives, on_device(): grad_short, grad_skip = lax.psum((short_terms, skip_terms), 'seq')  252 us
    dot_general x36, matrix products, along_rows(): return jnp.tensordot(factor, values, axes=1, precision=exact_mode)  58.4 us
    unnamed x53, local copies, waits for them, and re-layouts  20.7 us
    all_to_all x1, starting transfers between devices, on_device(): lax.all_to_all(grad_pair[0][None].astype(jnp.bfloat16), 'seq', split_axis...  12.3 us
  transfers between devices with their start and end apart: 19, of which 13 were waited for; matrix products, arithmetic and copies ran while one was open for 18% of the time, Pallas kernels for 0%

commit v1 on v0

--- a/solution.py
+++ b/solution.py
@@ -99,7 +99,15 @@
         lax.all_to_all(input_pair[0][None], "seq", split_axis=1, concat_axis=0, tiled=True),
         lax.all_to_all(input_pair[1][None], "seq", split_axis=1, concat_axis=0, tiled=True),
         lax.all_to_all(filter_pair[0][None], "seq", split_axis=1, concat_axis=0, tiled=True),
-        lax.all_to_all(filter_pair[1][None], "seq", split_axis=1, concat_axis=0, tiled=True),
+        jnp.concatenate(
+            lax.all_to_all(
+                jnp.stack(jnp.split(filter_pair[1][None], lax.axis_size("seq"), axis=1)),
+                "seq",
+                0,
+                0,
+            ),
+            axis=0,
+        ),
     )
     input_spectrum = block_forward((moved_data[0], moved_data[1]), block_basis)
     filter_spectrum = block_forward((moved_data[2], moved_data[3]), block_basis)

time: 606 us -> 644 us (1.063)
  local copies, waits for them, and re-layouts: 47.8 us -> 85.3 us
    unnamed x53 -> x116, local copies, waits for them, and re-layouts: 20.7 us -> 58.3 us
  transfers between devices with their start and end apart: 19 -> 19, of which waited for: 13 -> 12; matrix products, arithmetic and copies ran while one was open for 18% -> 17% of each run, Pallas kernels for 0% -> 0%
where the time goes in v1:
time: 644 us; the launch traced here: 634 us
  blocking collectives  252 us (39%)
  starting transfers between devices  123 us (19%)
  local copies, waits for them, and re-layouts  85.3 us (13%)
  waiting for transfers between devices  70.8 us (11%)
  matrix products  70.6 us (11%)
  other arithmetic  17.5 us (3%)
  between operations  14.8 us (2%)
    psum x1, blocking collectives, on_device(): grad_short, grad_skip = lax.psum((short_terms, skip_terms), 'seq')  252 us
    dot_general x36, matrix products, along_rows(): return jnp.tensordot(factor, values, axes=1, precision=exact_mode)  58.4 us
    unnamed x116, local copies, waits for them, and re-layouts  58.3 us
  transfers between devices with their start and end apart: 19, of which 12 were waited for; matrix products, arithmetic and copies ran while one was open for 17% of the time, Pallas kernels for 0%

profile of v1, /device:TPU:128, one launch (start us, length us, event | category | flops | bytes accessed | tf_op | source)
XLA Modules:
  0.0 633.9 jit_solution(16280565844736758536)
XLA Ops:
  47.3 10.5 %all-to-all-start.1 = ((f32[64,1,4,512]{3,2,1,0:T(4,128)}), f32[64,1,4,512]{3,2,1,0:T(4,128)S(1)}, u32[]{:S(2)}, u32[]{:S(2)}) async-start(f32[64,1,4,512]{3,2,1,0:T(4,128)} %constant_dynamic-update-slice_fusion), calls=%async_computation.1 | async-start | bytes 1048576 | tf_op jit(solution)/shard_map/all_to_all | solution.py:103
  59.3 2.1 collective-permute-start
  63.8 8.9 %all-to-all-done.1 = f32[64,1,4,512]{3,2,1,0:T(4,128)S(1)} async-done(((f32[64,1,4,512]{3,2,1,0:T(4,128)}), f32[64,1,4,512]{3,2,1,0:T(4,128)S(1)}, u32[]{:S(2)}, u32[]{:S(2)}) %all-to-all-start.1) | async-done | bytes 524320 | tf_op jit(solution)/shard_map/all_to_all | solution.py:103
  72.7 8.6 %all-to-all-start = ((f32[1,256,512]{2,0,1:T(1,128)}), f32[1,256,512]{2,0,1:T(1,128)S(1)}, u32[]{:S(2)}, u32[]{:S(2)}) async-start(f32[1,256,512]{2,0,1:T(1,128)} %copy.64), calls=%async_computation | async-start | bytes 1048576 | tf_op jit(solution)/shard_map/all_to_all | solution.py:101
  81.7 6.6 %all-gather.2.cloned.1.call-done = bf16[128,4096]{1,0:T(8,128)(2,1)} async-done(((bf16[128,1024]{1,0:T(8,128)(2,1)}), bf16[128,4096]{1,0:T(8,128)(2,1)}) %all-gather.2.cloned.1.call-update) | async-done | bytes 1048592 | tf_op jit(solution)/shard_map/all_gather | solution.py:128
  88.3 4.8 multiply_reduce_fusion.3
  93.1 3.1 collective-permute-start.2
  96.2 2.5 collective-permute-done.2
  99.4 1.6 fusion.14
  102.8 3.1 reduce.7
  106.8 12.0 %all-to-all-start.6 = ((bf16[64,2,1024]{2,1,0:T(2,128)(2,1)}), bf16[64,2,1024]{2,1,0:T(2,128)(2,1)S(1)}, u32[]{:S(2)}, u32[]{:S(2)}) async-start(bf16[64,2,1024]{2,1,0:T(2,128)(2,1)} %reshape.75), calls=%async_computation.7 | async-start | bytes 524288 | tf_op jit(solution)/shard_map/all_to_all | solution.py:149
  118.8 2.2 reduce
  122.1 2.6 fusion.15
  125.1 2.2 reduce.8
  128.2 10.3 %all-to-all-start.7 = ((bf16[64,2,1024]{2,1,0:T(2,128)(2,1)}), bf16[64,2,1024]{2,1,0:T(2,128)(2,1)S(1)}, u32[]{:S(2)}, u32[]{:S(2)}) async-start(bf16[64,2,1024]{2,1,0:T(2,128)(2,1)} %reshape.73), calls=%async_computation.8 | async-start | bytes 524288 | tf_op jit(solution)/shard_map/all_to_all | solution.py:152
  139.7 2.1 convolution_add_fusion.2
  144.2 3.5 all-to-all-done.7
  147.8 8.9 %all-to-all-start.3 = ((f32[1,256,512]{2,0,1:T(1,128)}), f32[1,256,512]{2,0,1:T(1,128)S(1)}, u32[]{:S(2)}, u32[]{:S(2)}) async-start(f32[1,256,512]{2,0,1:T(1,128)} %copy.69), calls=%async_computation.3 | async-start | bytes 1048576 | tf_op jit(solution)/shard_map/all_to_all | solution.py:100
  157.9 2.2 convolution_subtract_fusion.2
  162.5 2.1 reshape.76
  164.6 1.5 bitcast_reduce_fusion
  166.2 2.1 reshape.74
  168.3 1.5 bitcast_reduce_fusion.1
  169.9 1.5 all-to-all-done.3
  171.4 9.0 %all-to-all-start.2 = ((f32[1,256,512]{2,0,1:T(1,128)}), f32[1,256,512]{2,0,1:T(1,128)S(1)}, u32[]{:S(2)}, u32[]{:S(2)}) async-start(f32[1,256,512]{2,0,1:T(1,128)} %copy.67), calls=%async_computation.2 | async-start | bytes 1048576 | tf_op jit(solution)/shard_map/all_to_all | solution.py:99
  182.0 1.7 convolution_subtract_fusion
  183.7 1.7 convolution_add_fusion
  186.8 8.3 %all-to-all-done.2 = f32[1,256,512]{2,0,1:T(1,128)S(1)} async-done(((f32[1,256,512]{2,0,1:T(1,128)}), f32[1,256,512]{2,0,1:T(1,128)S(1)}, u32[]{:S(2)}, u32[]{:S(2)}) %all-to-all-start.2) | async-done | bytes 524320 | tf_op jit(solution)/shard_map/all_to_all | solution.py:99
  200.1 5.8 multiply_subtract_fusion
  209.8 8.7 %all-to-all-start.8 = ((bf16[64,4,512]{2,1,0:T(4,128)(2,1)}), bf16[64,4,512]{2,1,0:T(4,128)(2,1)}, u32[]{:S(2)}, u32[]{:S(2)}) async-start(bf16[64,4,512]{2,1,0:T(4,128)(2,1)} %copy.83), calls=%async_computation.9 | async-start | bytes 524288 | tf_op jit(solution)/shard_map/all_to_all | solution.py:160
  218.6 2.0 fusion.115
  220.6 2.0 fusion.5
  223.8 4.0 all-to-all-done.8
  227.7 9.1 %all-to-all-start.4 = ((f32[64,4,512]{2,1,0:T(4,128)}), f32[64,4,512]{2,1,0:T(4,128)}, u32[]{:S(2)}, u32[]{:S(2)}) async-start(f32[64,4,512]{2,1,0:T(4,128)} %copy.75), calls=%async_computation.4 | async-start | bytes 1048576 | tf_op jit(solution)/shard_map/all_to_all | solution.py:116
  236.9 2.0 fusion.113
  238.9 2.0 fusion.4
  242.1 9.7 %all-to-all-done.4 = f32[64,4,512]{2,1,0:T(4,128)} async-done(((f32[64,4,512]{2,1,0:T(4,128)}), f32[64,4,512]{2,1,0:T(4,128)}, u32[]{:S(2)}, u32[]{:S(2)}) %all-to-all-start.4) | async-done | bytes 524320 | tf_op jit(solution)/shard_map/all_to_all | solution.py:116
  251.7 8.7 %all-to-all-start.5 = ((f32[64,4,512]{2,1,0:T(4,128)}), f32[64,4,512]{2,1,0:T(4,128)}, u32[]{:S(2)}, u32[]{:S(2)}) async-start(f32[64,4,512]{2,1,0:T(4,128)} %copy.76), calls=%async_computation.5 | async-start | bytes 1048576 | tf_op jit(solution)/shard_map/all_to_all | solution.py:117
  261.2 2.0 fusion.11
  264.2 1.7 squeeze.41
  265.9 2.1 squeeze.39
  268.0 7.2 %all-to-all-done.5 = f32[64,4,512]{2,1,0:T(4,128)} async-done(((f32[64,4,512]{2,1,0:T(4,128)}), f32[64,4,512]{2,1,0:T(4,128)}, u32[]{:S(2)}, u32[]{:S(2)}) %all-to-all-start.5) | async-done | bytes 524320 | tf_op jit(solution)/shard_map/all_to_all | solution.py:117
  275.2 8.7 %all-to-all-start.9 = ((bf16[64,4,512]{2,1,0:T(4,128)(2,1)}), bf16[64,4,512]{2,1,0:T(4,128)(2,1)}, u32[]{:S(2)}, u32[]{:S(2)}) async-start(bf16[64,4,512]{2,1,0:T(4,128)(2,1)} %copy.84), calls=%async_computation.10 | async-start | bytes 524288 | tf_op jit(solution)/shard_map/all_to_all | solution.py:161
  284.2 3.5 fusion.61
  287.7 2.0 squeeze.40
  289.7 2.8 fusion.8
  294.1 2.0 collective-permute-start.1
  296.2 2.4 fusion.71
  298.6 1.7 squeeze.42
  300.3 1.9 fusion.18
  302.3 3.2 collective-permute-done.1
  305.4 1.8 multiply_bitcast_fusion.2
  308.1 2.0 fusion.301
  310.2 5.4 convolution_bitcast_fusion
  315.6 9.1 %copy.89 = f32[4096,512]{1,0:T(8,128)} copy(f32[4096,512]{0,1:T(8,128)} %convolution_bitcast_fusion) | data formatting | bytes 16777216
  327.6 8.5 %all-to-all-start.11 = ((bf16[64,4,512]{2,1,0:T(4,128)(2,1)}), bf16[64,4,512]{2,1,0:T(4,128)(2,1)}, u32[]{:S(2)}, u32[]{:S(2)}) async-start(bf16[64,4,512]{2,1,0:T(4,128)(2,1)} %copy.86), calls=%async_computation.12 | async-start | bytes 524288 | tf_op jit(solution)/shard_map/all_to_all | solution.py:163
  338.7 6.4 %all-to-all-done.11 = bf16[64,4,512]{2,1,0:T(4,128)(2,1)} async-done(((bf16[64,4,512]{2,1,0:T(4,128)(2,1)}), bf16[64,4,512]{2,1,0:T(4,128)(2,1)}, u32[]{:S(2)}, u32[]{:S(2)}) %all-to-all-start.11) | async-done | bytes 262176 | tf_op jit(solution)/shard_map/all_to_all | solution.py:163
  345.1 8.6 %all-to-all-start.10 = ((bf16[64,4,512]{2,1,0:T(4,128)(2,1)}), bf16[64,4,512]{2,1,0:T(4,128)(2,1)S(1)}, u32[]{:S(2)}, u32[]{:S(2)}) async-start(bf16[64,4,512]{2,1,0:T(4,128)(2,1)} %copy.85), calls=%async_computation.11 | async-start | bytes 524288 | tf_op jit(solution)/shard_map/all_to_all | solution.py:162
  354.8 8.2 %all-to-all-done.10 = bf16[64,4,512]{2,1,0:T(4,128)(2,1)S(1)} async-done(((bf16[64,4,512]{2,1,0:T(4,128)(2,1)}), bf16[64,4,512]{2,1,0:T(4,128)(2,1)S(1)}, u32[]{:S(2)}, u32[]{:S(2)}) %all-to-all-start.10) | async-done | bytes 262176 | tf_op jit(solution)/shard_map/all_to_all | solution.py:162
  364.0 4.2 collective-permute-start.3
  368.2 1.5 fusion.16
  370.7 1.5 multiply_reduce_fusion.2
  372.2 251.6 %all-reduce = (f32[3,3,512]{2,0,1:T(4,128)S(1)}, f32[512]{0:T(512)}) all-reduce(f32[3,3,512]{2,0,1:T(4,128)S(1)} %pad_maximum_fusion.5, f32[512]{0:T(512)S(1)} %get-tuple-element.45), channel_id=1, replica_groups=mesh['seq'=64,'ch'=4] {'seq'}, use_global_device_ids=true, to_apply=%region_4.5 | all-reduce | flops 5120 | bytes 40960 | tf_op jit(solution)/shard_map/psum | solution.py:183
  625.4 1.8 convert_element_type.124
  (179 shorter events, 85.6 us)
Async XLA Ops:
  7.2 1.0 copy-start
  7.2 74.1 %copy-start.16 = (bf16[128,512]{1,0:T(8,128)(2,1)S(1)}, bf16[128,512]{1,0:T(8,128)(2,1)}, u32[]{:S(2)}) copy-start(bf16[128,512]{1,0:T(8,128)(2,1)} %param.10) | copy-start | bytes 393220
  7.2 74.1 %copy-start.17 = (bf16[128,512]{1,0:T(8,128)(2,1)S(1)}, bf16[128,512]{1,0:T(8,128)(2,1)}, u32[]{:S(2)}) copy-start(bf16[128,512]{1,0:T(8,128)(2,1)} %param.9) | copy-start | bytes 393220
  7.2 74.1 %copy-start.18 = (bf16[128,512]{1,0:T(8,128)(2,1)S(1)}, bf16[128,512]{1,0:T(8,128)(2,1)}, u32[]{:S(2)}) copy-start(bf16[128,512]{1,0:T(8,128)(2,1)} %param.8) | copy-start | bytes 393220
  7.2 56.6 %copy-start.20 = (f32[3,3,512]{2,1,0:T(4,128)S(1)}, f32[3,3,512]{2,1,0:T(4,128)}, u32[]{:S(2)}) copy-start(f32[3,3,512]{2,1,0:T(4,128)} %param.11) | copy-start | bytes 55300
  47.3 25.4 %all-to-all-start.1 = ((f32[64,1,4,512]{3,2,1,0:T(4,128)}), f32[64,1,4,512]{3,2,1,0:T(4,128)S(1)}, u32[]{:S(2)}, u32[]{:S(2)}) async-start(f32[64,1,4,512]{3,2,1,0:T(4,128)} %constant_dynamic-update-slice_fusion), calls=%async_computation.1 | async-start | bytes 1048576 | tf_op jit(solution)/shard_map/all_to_all | solution.py:103
  57.8 30.5 %all-gather.2.cloned.1.call-start = ((), (), s32[]{:S(2)}) async-start(), calls=%async_computation.15 | async-start | bytes 1310720 | tf_op jit(solution)/shard_map/all_gather | solution.py:128
  59.3 22.0 %collective-permute-start = (bf16[3,2,512]{2,1,0:T(2,128)(2,1)S(1)}, bf16[3,2,512]{2,1,0:T(2,128)(2,1)S(1)}, u32[]{:S(2)}, u32[]{:S(2)}) collective-permute-start(bf16[3,2,512]{2,1,0:T(2,128)(2,1)S(1)} %pad_maximum_fusion.6), channel_id=1, source_target_pairs={{0,4},{4,8},{8,12},{12,16},{16,20},{20,24},{24,28},{28,32},{32,36}... | collective-permute-start | bytes 18440 | tf_op jit(solution)/shard_map/ppermute | solution.py:13
  72.7 34.1 %all-to-all-start = ((f32[1,256,512]{2,0,1:T(1,128)}), f32[1,256,512]{2,0,1:T(1,128)S(1)}, u32[]{:S(2)}, u32[]{:S(2)}) async-start(f32[1,256,512]{2,0,1:T(1,128)} %copy.64), calls=%async_computation | async-start | bytes 1048576 | tf_op jit(solution)/shard_map/all_to_all | solution.py:101
  81.7 19.3 %copy-start.6 = (f32[3,128,512]{2,1,0:T(8,128)}, f32[3,128,512]{2,1,0:T(8,128)S(1)}, u32[]{:S(2)}) copy-start(f32[3,128,512]{2,1,0:T(8,128)S(1)} %multiply_add_fusion.3) | copy-start | bytes 2359300
  93.1 5.6 collective-permute-start.2
  98.7 0.7 copy-start.19
  106.8 21.4 %all-to-all-start.6 = ((bf16[64,2,1024]{2,1,0:T(2,128)(2,1)}), bf16[64,2,1024]{2,1,0:T(2,128)(2,1)S(1)}, u32[]{:S(2)}, u32[]{:S(2)}) async-start(bf16[64,2,1024]{2,1,0:T(2,128)(2,1)} %reshape.75), calls=%async_computation.7 | async-start | bytes 524288 | tf_op jit(solution)/shard_map/all_to_all | solution.py:149
  128.2 29.7 %copy-start.13 = (bf16[64,2,1024]{2,1,0:T(2,128)(2,1)}, bf16[64,2,1024]{2,1,0:T(2,128)(2,1)S(1)}, u32[]{:S(2)}) copy-start(bf16[64,2,1024]{2,1,0:T(2,128)(2,1)S(1)} %all-to-all-done.6) | copy-start | bytes 786436
  128.2 19.5 %all-to-all-start.7 = ((bf16[64,2,1024]{2,1,0:T(2,128)(2,1)}), bf16[64,2,1024]{2,1,0:T(2,128)(2,1)S(1)}, u32[]{:S(2)}, u32[]{:S(2)}) async-start(bf16[64,2,1024]{2,1,0:T(2,128)(2,1)} %reshape.73), calls=%async_computation.8 | async-start | bytes 524288 | tf_op jit(solution)/shard_map/all_to_all | solution.py:152
  147.8 10.1 %copy-start.14 = (bf16[64,2,1024]{2,1,0:T(2,128)(2,1)}, bf16[64,2,1024]{2,1,0:T(2,128)(2,1)S(1)}, u32[]{:S(2)}) copy-start(bf16[64,2,1024]{2,1,0:T(2,128)(2,1)S(1)} %all-to-all-done.7) | copy-start | bytes 786436
  147.8 23.7 %all-to-all-start.3 = ((f32[1,256,512]{2,0,1:T(1,128)}), f32[1,256,512]{2,0,1:T(1,128)S(1)}, u32[]{:S(2)}, u32[]{:S(2)}) async-start(f32[1,256,512]{2,0,1:T(1,128)} %copy.69), calls=%async_computation.3 | async-start | bytes 1048576 | tf_op jit(solution)/shard_map/all_to_all | solution.py:100
  171.4 23.7 %all-to-all-start.2 = ((f32[1,256,512]{2,0,1:T(1,128)}), f32[1,256,512]{2,0,1:T(1,128)S(1)}, u32[]{:S(2)}, u32[]{:S(2)}) async-start(f32[1,256,512]{2,0,1:T(1,128)} %copy.67), calls=%async_computation.2 | async-start | bytes 1048576 | tf_op jit(solution)/shard_map/all_to_all | solution.py:99
  196.5 2.4 copy-start.5
  205.9 1.0 copy-start.4
  209.8 17.9 %all-to-all-start.8 = ((bf16[64,4,512]{2,1,0:T(4,128)(2,1)}), bf16[64,4,512]{2,1,0:T(4,128)(2,1)}, u32[]{:S(2)}, u32[]{:S(2)}) async-start(bf16[64,4,512]{2,1,0:T(4,128)(2,1)} %copy.83), calls=%async_computation.9 | async-start | bytes 524288 | tf_op jit(solution)/shard_map/all_to_all | solution.py:160
  227.7 24.0 %all-to-all-start.4 = ((f32[64,4,512]{2,1,0:T(4,128)}), f32[64,4,512]{2,1,0:T(4,128)}, u32[]{:S(2)}, u32[]{:S(2)}) async-start(f32[64,4,512]{2,1,0:T(4,128)} %copy.75), calls=%async_computation.4 | async-start | bytes 1048576 | tf_op jit(solution)/shard_map/all_to_all | solution.py:116
  251.7 23.5 %all-to-all-start.5 = ((f32[64,4,512]{2,1,0:T(4,128)}), f32[64,4,512]{2,1,0:T(4,128)}, u32[]{:S(2)}, u32[]{:S(2)}) async-start(f32[64,4,512]{2,1,0:T(4,128)} %copy.76), calls=%async_computation.5 | async-start | bytes 1048576 | tf_op jit(solution)/shard_map/all_to_all | solution.py:117
  263.3 37.0 %copy-start.21 = (f32[512]{0:T(512)S(1)}, f32[512]{0:T(512)}, u32[]{:S(2)}) copy-start(f32[512]{0:T(512)} %param.13) | copy-start | bytes 6148
  265.9 39.5 %copy-start.15 = (f32[128,512]{1,0:T(8,128)S(1)}, f32[128,512]{1,0:T(8,128)}, u32[]{:S(2)}) copy-start(f32[128,512]{1,0:T(8,128)} %get-tuple-element.70) | copy-start | bytes 786436
  275.2 23.4 %all-to-all-start.9 = ((bf16[64,4,512]{2,1,0:T(4,128)(2,1)}), bf16[64,4,512]{2,1,0:T(4,128)(2,1)}, u32[]{:S(2)}, u32[]{:S(2)}) async-start(bf16[64,4,512]{2,1,0:T(4,128)(2,1)} %copy.84), calls=%async_computation.10 | async-start | bytes 524288 | tf_op jit(solution)/shard_map/all_to_all | solution.py:161
  284.0 23.3 %copy-start.7 = (f32[3,128,512]{2,1,0:T(8,128)S(1)}, f32[3,128,512]{2,1,0:T(8,128)}, u32[]{:S(2)}) copy-start(f32[3,128,512]{2,1,0:T(8,128)} %copy-done.6) | copy-start | bytes 2359300
  284.0 341.4 %reduce-scatter.5.cloned.1.call-start = ((), (), s32[]{:S(2)}) async-start(), calls=%async_computation.14 | async-start | bytes 2621440 | tf_op jit(solution)/shard_map/reduce_scatter | solution.py:125
  292.6 0.8 copy-start.11
  294.1 11.3 %collective-permute-start.1 = (f32[128,512]{1,0:T(8,128)}, f32[128,512]{1,0:T(8,128)}, u32[]{:S(2)}, u32[]{:S(2)}) collective-permute-start(f32[128,512]{1,0:T(8,128)} %slice.82), channel_id=1, source_target_pairs={{0,4},{4,8},{8,12},{12,16},{16,20},{20,24},{24,28},{28,32},{32,36}... | collective-permute-start | bytes 786440 | tf_op jit(solution)/shard_map/ppermute | solution.py:13
  300.3 7.8 %copy-start.2 = (bf16[512,4096]{1,0:T(8,128)(2,1)S(1)}, bf16[512,4096]{1,0:T(8,128)(2,1)}, u32[]{:S(2)}) copy-start(bf16[512,4096]{1,0:T(8,128)(2,1)} %param.14) | copy-start | bytes 12582916
  307.4 0.7 copy-start.12
  307.4 56.4 %copy-start.9 = (f32[1,128,512]{2,1,0:T(8,128)}, f32[1,128,512]{2,1,0:T(8,128)S(1)}, u32[]{:S(2)}) copy-start(f32[1,128,512]{2,1,0:T(8,128)S(1)} %get-tuple-element.61) | copy-start | bytes 786436
  308.1 2.1 copy-start.8
  310.1 317.0 %reduce-scatter.7.cloned.1.call-start = ((), (), s32[]{:S(2)}) async-start(), calls=%async_computation.16 | async-start | bytes 8519680
  324.7 1.2 copy-start.3
  327.6 17.5 %all-to-all-start.11 = ((bf16[64,4,512]{2,1,0:T(4,128)(2,1)}), bf16[64,4,512]{2,1,0:T(4,128)(2,1)}, u32[]{:S(2)}, u32[]{:S(2)}) async-start(bf16[64,4,512]{2,1,0:T(4,128)(2,1)} %copy.86), calls=%async_computation.12 | async-start | bytes 524288 | tf_op jit(solution)/shard_map/all_to_all | solution.py:163
  337.0 26.9 %copy-start.10 = (f32[1,128,512]{2,1,0:T(8,128)S(1)}, f32[1,128,512]{2,1,0:T(8,128)}, u32[]{:S(2)}) copy-start(f32[1,128,512]{2,1,0:T(8,128)} %get-tuple-element.48) | copy-start | bytes 786436
  345.1 17.9 %all-to-all-start.10 = ((bf16[64,4,512]{2,1,0:T(4,128)(2,1)}), bf16[64,4,512]{2,1,0:T(4,128)(2,1)S(1)}, u32[]{:S(2)}, u32[]{:S(2)}) async-start(bf16[64,4,512]{2,1,0:T(4,128)(2,1)} %copy.85), calls=%async_computation.11 | async-start | bytes 524288 | tf_op jit(solution)/shard_map/all_to_all | solution.py:162
  364.0 5.7 collective-permute-start.3
  369.6 257.5 %copy-start.1 = (f32[128,512]{1,0:T(8,128)S(1)}, f32[128,512]{1,0:T(8,128)}, u32[]{:S(2)}) copy-start(f32[128,512]{1,0:T(8,128)} %param.12) | copy-start | bytes 786436
Sparse Core Ops, SparseCore 0:
  60.5 27.7 all-gather.1
  310.3 30.2 reduce-scatter.4
  345.9 149.4 reduce-scatter.6
